TPU v7x, 32 devices: a whole 2x2x4 slice. The times are simulated.
32 devices in a mesh: freq: 4 (over z), pts: 8 (over y, x, core).
Axes of the slice: x: 2, y: 2, z: 4, core: 2. Of those that a mesh axis runs over, the one named last changes fastest.
Arguments:
- histories: float32 [8, 2048, 4096], P(None, ('freq', 'pts')), may hold values from -6 to 6
- point_weight: float32 [4096], P('pts'), may hold values from 0.5 to 2
- basis: float32 [4096, 4096], P('pts', 'freq'), may hold values from -0.09375 to 0.09375
Outputs:
- coeffs: float32 [8, 2, 256, 4096], P(None, None, 'freq', 'pts')
All inputs are finite; a program needn't handle non-finite values.
Results may differ from a plain program's by a relative error of at most 0.00011.
Values sent between devices are 32-bit elements; how exact they have to be, the bound alone decides.
A program may use at most 128 MiB of HBM per device.

v0:
```python
import functools

import jax
import jax.numpy as jnp
from jax import lax
from jax.experimental import pallas as pl
from jax.experimental.pallas import tpu as pltpu
from jax.sharding import PartitionSpec as P

F = 256
LEAD = 2
AHEAD = 8
COLS = 128
RING = 2
MESH = pl.DeviceIdType.MESH


def make_table(times, total, bins, blocks):
    freqs = jnp.arange(1, bins + 1, dtype=jnp.int32)
    phase_int = freqs[:, None] * times[None, :] % total
    angle = 2.0 * jnp.pi / total * phase_int.astype(jnp.float32)
    window = 0.5 - 0.5 * jnp.cos(2.0 * jnp.pi / total * times.astype(jnp.float32))
    scale = (window / jnp.sqrt(jnp.float32(total)))[None, :]
    cos = (jnp.cos(angle) * scale).reshape(blocks, 1, bins // blocks, -1)
    sin = (-jnp.sin(angle) * scale).reshape(blocks, 1, bins // blocks, -1)
    return jnp.concatenate([cos, sin], axis=1).reshape(2 * bins, -1)


def split(x):
    high = x.astype(jnp.bfloat16)
    return high, (x - high.astype(jnp.float32)).astype(jnp.bfloat16)


def dot3(a, b):
    ah, al = a
    bh, bl = b
    dot = functools.partial(jnp.dot, preferred_element_type=jnp.float32)
    return dot(ah, bh) + (dot(ah, bl) + dot(al, bh))


def kernel(
    nf, np_, hist, table, weight, basis, out,
    h2, bas, rs, spec, wf, th, tl_, wh, wl, cown, csend, pland, fland,
    h_send, h_recv, h_own, b_send_r, b_send_l, b_recv, b_own,
    r_send, r_recv, p_send, p_recv, f_send, f_recv, o_sem,
):
    cases, time_local, _ = hist.shape
    points = h2.shape[2]
    rows = wh.shape[1]
    per = np_ // nf
    pieces = bas.shape[1]
    ho = pieces * COLS
    chunks = per * pieces
    chips = np_ // 2
    me = lax.axis_index("freq")
    p = lax.axis_index("pts")
    core = lax.rem(p, 2)
    chip = lax.div(p, 2)
    right, left = jnp.minimum(me + 1, nf - 1), jnp.maximum(me - 1, 0)
    has_r, has_l = me < nf - 1, me > 0

    barrier = pltpu.get_barrier_semaphore()
    for d in range(1, np_):
        pl.semaphore_signal(barrier, inc=1, device_id={"pts": lax.rem(p + d, np_)}, device_id_type=MESH)

    @pl.when(has_r)
    def _():
        pl.semaphore_signal(barrier, inc=1, device_id={"freq": right}, device_id_type=MESH)

    @pl.when(has_l)
    def _():
        pl.semaphore_signal(barrier, inc=1, device_id={"freq": left}, device_id_type=MESH)

    inner = jnp.logical_and(has_l, has_r)

    @pl.when(inner)
    def _():
        pl.semaphore_wait(barrier, np_ + 1)

    @pl.when(jnp.logical_not(inner))
    def _():
        pl.semaphore_wait(barrier, np_)

    def h_copy(s, q, slot):
        return pltpu.make_async_remote_copy(
            src_ref=hist.at[s, :, pl.ds(pl.multiple_of(q * points, 128), points)],
            dst_ref=h2.at[s, pl.ds(pl.multiple_of(slot * time_local, 8), time_local), :],
            send_sem=h_send.at[s, q], recv_sem=h_recv.at[s, slot],
            device_id={"pts": q}, device_id_type=MESH,
        )

    def h_local(s):
        return pltpu.make_async_copy(
            hist.at[s, :, pl.ds(pl.multiple_of(p * points, 128), points)],
            h2.at[s, pl.ds(pl.multiple_of(p * time_local, 8), time_local), :],
            h_own.at[s],
        )

    def h_start(s):
        for d in range(1, np_):
            h_copy(s, lax.rem(p + d, np_), p).start()
        h_local(s).start()

    def b_source(n):
        at = lax.rem(n, per) * ho + lax.div(n, per) * COLS
        return basis.at[:, pl.ds(pl.multiple_of(at, 128), COLS)]

    def b_place(b, n):
        return bas.at[b * per + lax.rem(n, per), lax.div(n, per)]

    def b_copy(b, n, to, sems, src=None):
        dst = b_place(b, n)
        return pltpu.make_async_remote_copy(
            src_ref=dst if src is None else src, dst_ref=dst,
            send_sem=sems.at[b, n], recv_sem=b_recv.at[b, n],
            device_id={"freq": to}, device_id_type=MESH,
        )

    def b_local(n):
        return pltpu.make_async_copy(b_source(n), b_place(me, n), b_own.at[n])

    def r_copy(s, g, dst, to):
        return pltpu.make_async_remote_copy(
            src_ref=rs.at[s, g], dst_ref=rs.at[s, dst], send_sem=r_send.at[s, g], recv_sem=r_recv.at[s, dst],
            device_id={"freq": to}, device_id_type=MESH,
        )

    def own(s, g):
        return spec[lax.rem(s, RING), pl.ds(pl.multiple_of(g * rows, 8), rows), :]

    def place_in(t, hops):
        u = t - 2 * hops + nf * (LEAD + 2)
        return lax.div(u, nf) - (LEAD + 2), lax.rem(u, nf)

    def forward(k, g, behind, ahead, has_ahead, to, sems, last):
        n = k + LEAD
        sums = jnp.logical_and(jnp.logical_and(has_ahead, ahead), jnp.logical_and(k >= 0, k < cases))

        @pl.when(sums)
        def _():
            @pl.when(behind)
            def _():
                r_copy(k, g, g, to).wait_recv()
                rs[k, g] = rs[k, g] + own(k, g)

            @pl.when(jnp.logical_not(behind))
            def _():
                rs[k, g] = own(k, g)

            if last is None:
                r_copy(k, g, g, to).start()
            else:
                @pl.when(last)
                def _():
                    r_copy(k, g, nf, to).start()

                @pl.when(jnp.logical_not(last))
                def _():
                    r_copy(k, g, g, to).start()

        chunk = jnp.logical_and(jnp.logical_not(ahead), jnp.logical_and(n >= 0, n < chunks))

        @pl.when(jnp.logical_and(chunk, g == me))
        def _():
            @pl.when(has_ahead)
            def _():
                b_copy(me, n, to, sems, b_source(n)).start()

        @pl.when(jnp.logical_and(chunk, g != me))
        def _():
            copy = b_copy(g, n, to, sems)
            copy.wait_recv()

            @pl.when(has_ahead)
            def _():
                copy.start()

    def send(t):
        k, r = place_in(t, me)
        g = nf - 1 - r
        forward(k, g, has_l, g > me, has_r, right, b_send_r, None)
        k, g = place_in(t, nf - 1 - me)
        forward(k, g, has_r, g < me, has_l, left, b_send_l, g == me - 1)

    def finalize(s):
        wf[...] = own(s, me)

        @pl.when(has_l)
        def _():
            r_copy(s, me, me, right).wait_recv()
            wf[...] = wf[...] + rs[s, me]

        @pl.when(has_r)
        def _():
            r_copy(s, nf, nf, left).wait_recv()
            wf[...] = wf[...] + rs[s, nf]

        high, low = split(wf[...] * weight[...])
        wh[s] = high
        wl[s] = low

    def p_copy(e, slot):
        return pltpu.make_async_remote_copy(
            src_ref=csend.at[slot], dst_ref=pland.at[e],
            send_sem=p_send.at[slot], recv_sem=p_recv.at[e],
            device_id={"pts": chip * 2 + 1 - core}, device_id_type=MESH,
        )

    def f_copy(e, c, slot):
        return pltpu.make_async_remote_copy(
            src_ref=pland.at[e, c], dst_ref=fland.at[e, slot], send_sem=f_send.at[e, c], recv_sem=f_recv.at[e, slot],
            device_id={"pts": c * 2 + core}, device_id_type=MESH,
        )

    def o_copy(e):
        s, m = lax.div(e, pieces), lax.rem(e, pieces)
        return pltpu.make_async_copy(
            pland.at[e, chip],
            out.at[pl.ds(pl.multiple_of(s * rows, 8), rows), pl.ds(pl.multiple_of(m * COLS, 128), COLS)],
            o_sem.at[e],
        )

    def compute(s, m, slot):
        lhs = wh[s], wl[s]
        for d in range(1, chips + 1):
            c = lax.rem(chip + d, chips)
            pair = jnp.concatenate([bas[c * 2 + 1 - core, m], bas[c * 2 + core, m]], axis=1)
            both = dot3(lhs, split(pair))
            csend[slot, c] = both[:, :COLS]
            cown[slot, c] = both[:, COLS:]
        p_copy(s * pieces + m, slot).start()

    def pass_on(s, m, slot):
        e = s * pieces + m
        copy = p_copy(e, slot)
        copy.wait_recv()
        copy.wait_send()
        pland[e] = pland[e] + cown[slot]
        for d in range(1, chips):
            f_copy(e, lax.rem(chip + d, chips), chip).start()

    across = -(-pieces // nf)

    def ready(i):
        return jnp.minimum(lax.div(i + LEAD - 1, per), pieces)

    def units(t, act):
        v = t - (nf - 2) + nf * (LEAD + 2)
        i, part = lax.div(v, nf) - (LEAD + 2), lax.rem(v, nf)
        s = i - 1

        @pl.when(jnp.logical_and(s >= 0, s < cases))
        def _():
            done = ready(i)
            low = lax.div(part * pieces, nf)
            high = jnp.minimum(lax.div((part + 1) * pieces, nf), done)

            def new_case(m, carry):
                act(s, m, m - low)
                return carry

            lax.fori_loop(low, high, new_case, 0)
            m_new = ready(i - 1)

            @pl.when(done > m_new)
            def _():
                start = lax.div(part * s, nf)

                def new_piece(r, carry):
                    act(r, m_new, across + r - start)
                    return carry

                lax.fori_loop(start, lax.div((part + 1) * s, nf), new_piece, 0)

    for n in range(chunks):
        b_local(n).start()

    def begin(s, carry):
        h_start(s)
        return carry

    lax.fori_loop(0, min(AHEAD, cases), begin, 0)
    high, low = split(table[...])
    th[...] = high
    tl_[...] = low

    def tick(step, carry):
        t = step - nf * LEAD
        i = lax.div(step, nf) - LEAD
        tau = lax.rem(step, nf)

        @pl.when(jnp.logical_and(tau == 0, jnp.logical_and(i >= 0, i < cases)))
        def _():
            if AHEAD < cases:
                @pl.when(i + AHEAD < cases)
                def _():
                    h_start(i + AHEAD)
            for d in range(1, np_):
                q = lax.rem(p + d, np_)
                h_copy(i, q, q).wait_recv()
            h_local(i).wait()
            with jax.named_scope('dft'):
              spec[lax.rem(i, RING)] = dot3((th[...], tl_[...]), split(h2[i]))

        with jax.named_scope('send'):
            send(t)

        @pl.when(jnp.logical_and(tau == nf - 2, jnp.logical_and(i >= 1, i <= cases)))
        def _():
            @pl.when(i == 1)
            def _():
                for n in range(chunks):
                    b_local(n).wait()

            with jax.named_scope('finalize'):
                finalize(i - 1)

        with jax.named_scope('pass'):
            units(t - 1, pass_on)
        with jax.named_scope('fit'):
            units(t, compute)
        return carry

    lax.fori_loop(0, nf * (LEAD + cases + 2) - 1, tick, 0)

    total = cases * pieces

    def finish(e, carry):
        acc = pland[e, chip]
        for d in range(1, chips):
            c = lax.rem(chip + d, chips)
            f_copy(e, c, c).wait_recv()
            acc = acc + fland[e, c]
        pland[e, chip] = acc
        o_copy(e).start()
        return carry

    with jax.named_scope('finish'):
        lax.fori_loop(0, total, finish, 0)

    def drain(s, carry):
        for d in range(1, np_):
            h_copy(s, lax.rem(p + d, np_), p).wait_send()
        for d in range(1, nf):
            @pl.when(me + d <= nf - 1)
            def _():
                r_copy(s, me + d, me + d, right).wait_send()

            @pl.when(me - d >= 0)
            def _():
                r_copy(s, me - d, me - d, left).wait_send()
        return carry

    lax.fori_loop(0, cases, drain, 0)
    for g in range(nf):
        @pl.when(jnp.logical_and(g <= me, has_r))
        def _():
            for n in range(chunks):
                b_copy(g, n, right, b_send_r).wait_send()

        @pl.when(jnp.logical_and(g >= me, has_l))
        def _():
            for n in range(chunks):
                b_copy(g, n, left, b_send_l).wait_send()

    def drain_out(e, carry):
        for d in range(1, chips):
            f_copy(e, lax.rem(chip + d, chips), chip).wait_send()
        o_copy(e).wait()
        return carry

    lax.fori_loop(0, total, drain_out, 0)


def local(histories, point_weight, basis):
    nf = lax.axis_size("freq")
    np_ = lax.axis_size("pts")
    cases, time_local, all_points = histories.shape
    points = all_points // np_
    plane_time = time_local * np_
    rows = 2 * F // nf
    ho = basis.shape[1] * nf // np_
    pieces = ho // COLS
    chunks = np_ // nf * pieces
    chips = np_ // 2
    total = cases * pieces
    slots = -(-pieces // nf) + -(-cases // nf)
    times = lax.axis_index("freq") * plane_time + jnp.arange(plane_time, dtype=jnp.int32)
    table = make_table(times, plane_time * nf, F, nf)
    f32, bf16 = jnp.float32, jnp.bfloat16
    hbm = pl.BlockSpec(memory_space=pl.ANY)
    vmem = pl.BlockSpec(memory_space=pltpu.VMEM)
    dma = pltpu.SemaphoreType.DMA
    coeffs = pl.pallas_call(
        functools.partial(kernel, nf, np_),
        out_shape=jax.ShapeDtypeStruct((cases * rows, ho), f32),
        in_specs=[hbm, vmem, vmem, hbm],
        out_specs=hbm,
        scratch_shapes=[
            pltpu.VMEM((cases, plane_time, points), f32),
            pltpu.VMEM((np_, pieces, points, COLS), f32),
            pltpu.VMEM((cases, nf + 1, rows, points), f32),
            pltpu.VMEM((RING, 2 * F, points), f32),
            pltpu.VMEM((rows, points), f32),
            pltpu.VMEM((2 * F, plane_time), bf16),
            pltpu.VMEM((2 * F, plane_time), bf16),
            pltpu.VMEM((cases, rows, points), bf16),
            pltpu.VMEM((cases, rows, points), bf16),
            pltpu.VMEM((slots, chips, rows, COLS), f32),
            pltpu.VMEM((slots, chips, rows, COLS), f32),
            pltpu.VMEM((total, chips, rows, COLS), f32),
            pltpu.VMEM((total, chips, rows, COLS), f32),
            dma((cases, np_)), dma((cases, np_)), dma((cases,)),
            dma((nf, chunks)), dma((nf, chunks)), dma((nf, chunks)), dma((chunks,)),
            dma((cases, nf)), dma((cases, nf + 1)),
            dma((slots,)), dma((total,)),
            dma((total, chips)), dma((total, chips)), dma((total,)),
        ],
        compiler_params=pltpu.CompilerParams(
            collective_id=0, has_side_effects=True, vmem_limit_bytes=60 * 1024 * 1024
        ),
    )(histories, table, point_weight.reshape(1, -1), basis)
    return coeffs.reshape(cases, 2, rows // 2, ho)


def solution(mesh):
    return jax.shard_map(
        local,
        mesh=mesh,
        in_specs=(P(None, ("freq", "pts"), None), P("pts"), P("pts", "freq")),
        out_specs=P(None, None, "freq", "pts"),
        check_vma=False,
    )
```

profile of v0, /device:TPU:1, one launch (start us, length us, event | category | flops | bytes accessed | tf_op | source)
XLA Modules:
  0.0 245.2 jit_solution(14509280808962189554)
XLA Ops:
  0.1 2.2 cosine_multiply_fusion
  2.2 1.0 pad_maximum_fusion
  3.3 238.8 %shard_map.37 = f32[1024,512]{1,0:T(8,128)} custom-call(f32[8,64,4096]{2,1,0:T(8,128)} %hist.1, f32[512,512]{1,0:T(8,128)} %bitcast.4, f32[1,512]{1,0:T(1,128)} %bitcast.5, f32[512,1024]{1,0:T(8,128)} %basis.1), custom_call_target="tpu_custom_call" | custom-call | tf_op jit(solution)/shard_map/pallas_call | solution.py:394
  242.1 3.1 %copy.5 = f32[8,2,64,512]{3,2,1,0:T(8,128)} copy(f32[8,2,64,512]{3,2,1,0:T(8,128)} %bitcast.3) | data formatting | bytes 4194304
  (3 shorter events, 0.1 us)
where the time goes:
time: 246 us; the launch traced here: 245 us
  Pallas kernels  239 us (97%)
  other arithmetic  3.27 us (1%)
  local copies, waits for them, and re-layouts  3.14 us (1%)
    pallas_call x1, Pallas kernels, local(): pl.pallas_call(functools.partial(kernel, nf, np_), out_shape=jax.ShapeDty...  239 us

commit v1 on v0

v1 whole, which is shorter than its diff:
```python
import functools
import math

import jax
import jax.numpy as jnp
from jax import lax
from jax.experimental import pallas as pl
from jax.experimental.pallas import tpu as pltpu
from jax.sharding import PartitionSpec as P

F = 256
LEAD = 2
LATE = 2
RELAY = 4
AHEAD = 8
COLS = 128
RING = 2
MESH = pl.DeviceIdType.MESH


def split(x):
    high = x.astype(jnp.bfloat16)
    return high, (x - high.astype(jnp.float32)).astype(jnp.bfloat16)


def dot3(a, b):
    ah, al = a
    bh, bl = b
    dot = functools.partial(jnp.dot, preferred_element_type=jnp.float32)
    return dot(ah, bh) + (dot(ah, bl) + dot(al, bh))


def kernel(
    nf, np_, hist, weight, basis, out,
    h2, bas, rs, spec, wf, th, tl_, wh, wl, stage, pland, fland,
    h_send, h_recv, h_own, b_send_r, b_send_l, b_recv, b_own,
    r_send, r_recv, p_send, p_recv, f_send, f_recv, o_sem,
):
    cases, time_local, _ = hist.shape
    points = h2.shape[2]
    rows = wh.shape[1]
    per = np_ // nf
    pieces = bas.shape[1]
    ho = pieces * COLS
    chunks = per * pieces
    chips = np_ // 2
    me = lax.axis_index("freq")
    p = lax.axis_index("pts")
    core = lax.rem(p, 2)
    chip = lax.div(p, 2)
    right, left = jnp.minimum(me + 1, nf - 1), jnp.maximum(me - 1, 0)
    has_r, has_l = me < nf - 1, me > 0

    barrier = pltpu.get_barrier_semaphore()
    for d in range(1, np_):
        pl.semaphore_signal(barrier, inc=1, device_id={"pts": lax.rem(p + d, np_)}, device_id_type=MESH)

    @pl.when(has_r)
    def _():
        pl.semaphore_signal(barrier, inc=1, device_id={"freq": right}, device_id_type=MESH)

    @pl.when(has_l)
    def _():
        pl.semaphore_signal(barrier, inc=1, device_id={"freq": left}, device_id_type=MESH)

    inner = jnp.logical_and(has_l, has_r)

    @pl.when(inner)
    def _():
        pl.semaphore_wait(barrier, np_ + 1)

    @pl.when(jnp.logical_not(inner))
    def _():
        pl.semaphore_wait(barrier, np_)

    def h_copy(s, q, slot):
        return pltpu.make_async_remote_copy(
            src_ref=hist.at[s, :, pl.ds(pl.multiple_of(q * points, 128), points)],
            dst_ref=h2.at[s, pl.ds(pl.multiple_of(slot * time_local, 8), time_local), :],
            send_sem=h_send.at[s, q], recv_sem=h_recv.at[s, slot],
            device_id={"pts": q}, device_id_type=MESH,
        )

    def h_local(s):
        return pltpu.make_async_copy(
            hist.at[s, :, pl.ds(pl.multiple_of(p * points, 128), points)],
            h2.at[s, pl.ds(pl.multiple_of(p * time_local, 8), time_local), :],
            h_own.at[s],
        )

    def h_start(s):
        for d in range(1, np_):
            h_copy(s, lax.rem(p + d, np_), p).start()
        h_local(s).start()

    def b_source(n):
        at = lax.rem(n, per) * ho + lax.div(n, per) * COLS
        return basis.at[:, pl.ds(pl.multiple_of(at, 128), COLS)]

    def b_place(b, n):
        return bas.at[b * per + lax.rem(n, per), lax.div(n, per)]

    def b_copy(b, n, to, sems, src=None):
        dst = b_place(b, n)
        return pltpu.make_async_remote_copy(
            src_ref=dst if src is None else src, dst_ref=dst,
            send_sem=sems.at[b, n], recv_sem=b_recv.at[b, n],
            device_id={"freq": to}, device_id_type=MESH,
        )

    def b_head(n):
        @pl.when(has_r)
        def _():
            b_copy(me, n, right, b_send_r, b_source(n)).start()

        @pl.when(has_l)
        def _():
            b_copy(me, n, left, b_send_l, b_source(n)).start()

    def b_local(n):
        return pltpu.make_async_copy(b_source(n), b_place(me, n), b_own.at[n])

    def r_copy(s, g, dst, to):
        return pltpu.make_async_remote_copy(
            src_ref=rs.at[s, g], dst_ref=rs.at[s, dst], send_sem=r_send.at[s, g], recv_sem=r_recv.at[s, dst],
            device_id={"freq": to}, device_id_type=MESH,
        )

    def own(s, g):
        return spec[lax.rem(s, RING), pl.ds(pl.multiple_of(g * rows, 8), rows), :]

    def place_in(t, hops):
        u = t - 2 * hops + nf * (LEAD + 2)
        return lax.div(u, nf) - (LEAD + 2), lax.rem(u, nf)

    def forward(k, g, behind, ahead, has_ahead, to, sems, last):
        sums = jnp.logical_and(jnp.logical_and(has_ahead, ahead), jnp.logical_and(k >= 0, k < cases))

        @pl.when(sums)
        def _():
            @pl.when(behind)
            def _():
                r_copy(k, g, g, to).wait_recv()
                rs[k, g] = rs[k, g] + own(k, g)

            @pl.when(jnp.logical_not(behind))
            def _():
                rs[k, g] = own(k, g)

            if last is None:
                r_copy(k, g, g, to).start()
            else:
                @pl.when(last)
                def _():
                    r_copy(k, g, nf, to).start()

                @pl.when(jnp.logical_not(last))
                def _():
                    r_copy(k, g, g, to).start()

        n = k + LEAD
        chunk = jnp.logical_and(jnp.logical_and(jnp.logical_not(ahead), has_ahead), jnp.logical_and(n >= 0, n < chunks))

        @pl.when(jnp.logical_and(chunk, jnp.logical_and(g == me, k >= 0)))
        def _():
            b_copy(me, n, to, sems, b_source(n)).start()

        @pl.when(jnp.logical_and(chunk, g != me))
        def _():
            copy = b_copy(g, n, to, sems)
            copy.wait_recv()
            copy.start()

    def send(t):
        k, r = place_in(t, me)
        g = nf - 1 - r
        forward(k, g, has_l, g > me, has_r, right, b_send_r, None)
        k, g = place_in(t, nf - 1 - me)
        forward(k, g, has_r, g < me, has_l, left, b_send_l, g == me - 1)

    def take(n):
        @pl.when(jnp.logical_not(has_r))
        def _():
            for b in range(nf - 1):
                b_copy(b, n, right, b_send_r).wait_recv()

        @pl.when(jnp.logical_not(has_l))
        def _():
            for b in range(1, nf):
                b_copy(b, n, left, b_send_l).wait_recv()

    def finalize(s):
        at = lax.rem(s, RING + 1)

        @pl.when(has_l)
        def _():
            r_copy(s, me, me, right).wait_recv()
            wf[at] = wf[at] + rs[s, me]

        @pl.when(has_r)
        def _():
            r_copy(s, nf, nf, left).wait_recv()
            wf[at] = wf[at] + rs[s, nf]

        high, low = split(wf[at] * weight[...])
        wh[s] = high
        wl[s] = low

    def p_copy(e, slot):
        return pltpu.make_async_remote_copy(
            src_ref=stage.at[slot], dst_ref=pland.at[e],
            send_sem=p_send.at[slot], recv_sem=p_recv.at[e],
            device_id={"pts": chip * 2 + 1 - core}, device_id_type=MESH,
        )

    lines = chips // 2
    cy, cx = lax.div(chip, 2), lax.rem(chip, 2)
    beside = cy * 2 + 1 - cx

    def f_copy(e, c, to, slot):
        return pltpu.make_async_remote_copy(
            src_ref=pland.at[e, c], dst_ref=fland.at[e, slot], send_sem=f_send.at[e, c], recv_sem=f_recv.at[e, slot],
            device_id={"pts": to * 2 + core}, device_id_type=MESH,
        )

    def landed(e, slot):
        f_copy(e, beside, beside, slot).wait_recv()
        return fland[e, slot]

    def others():
        return [lax.rem(cy + d, lines) for d in range(1, lines)]

    def o_copy(e):
        s, m = lax.div(e, pieces), lax.rem(e, pieces)
        return pltpu.make_async_copy(
            pland.at[e, chip],
            out.at[pl.ds(pl.multiple_of(s * rows, 8), rows), pl.ds(pl.multiple_of(m * COLS, 128), COLS)],
            o_sem.at[e],
        )

    def compute(s, n, slot):
        m, target = lax.div(n, 2), lax.rem(n, 2)
        lhs = wh[s], wl[s]
        for c in range(0, chips, 2):
            pair = jnp.concatenate([bas[c * 2 + target, m], bas[c * 2 + 2 + target, m]], axis=1)
            both = dot3(lhs, split(pair))
            stage[slot, c] = both[:, :COLS]
            stage[slot, c + 1] = both[:, COLS:]

        @pl.when(target != core)
        def _():
            p_copy(s * pieces + m, slot).start()

    def pass_on(s, n, slot):
        m, target = lax.div(n, 2), lax.rem(n, 2)

        @pl.when(target != core)
        def _():
            p_copy(s * pieces + m, slot).wait_send()

        @pl.when(target == core)
        def _():
            spread(s, m, slot)

    def spread(s, m, slot):
        e = s * pieces + m
        p_copy(e, slot).wait_recv()
        pland[e] = pland[e] + stage[slot]
        turn = lax.rem(s + m, 2)

        @pl.when(turn == 0)
        def _():
            for row in others() + [cy]:
                f_copy(e, row * 2 + 1 - cx, beside, row).start()

        @pl.when(turn == 1)
        def _():
            for row in others():
                f_copy(e, row * 2 + 1 - cx, row * 2 + cx, cy * 2 + 1).start()
                f_copy(e, row * 2 + cx, row * 2 + cx, cy * 2).start()

    def relay(s, n, slot):
        @pl.when(lax.rem(n, 2) == core)
        def _():
            turn_over(s, lax.div(n, 2))

    def turn_over(s, m):
        e = s * pieces + m
        turn = lax.rem(s + m, 2)

        @pl.when(turn == 0)
        def _():
            for row in others():
                c = row * 2 + cx
                pland[e, c] = pland[e, c] + landed(e, row)
                f_copy(e, c, c, lines + cy).start()

        @pl.when(turn == 1)
        def _():
            for row in others():
                pland[e, beside] = pland[e, beside] + landed(e, row * 2 + 1)
            f_copy(e, beside, beside, cy * 2).start()

    def ready(i):
        return jnp.minimum(i + LEAD - 1, chunks)

    def new_chunk(i, act):
        def cases_of(n, carry):
            def one(s, inner_carry):
                act(s, n, s)
                return inner_carry

            return lax.fori_loop(0, i - 1, one, carry)

        lax.fori_loop(ready(i - 1), ready(i), cases_of, 0)

    def new_case(i, act):
        def one(n, carry):
            act(i - 1, n, cases - 1 + n)
            return carry

        lax.fori_loop(0, ready(i), one, 0)

    between = jnp.minimum(me, 1) * jnp.minimum(nf - 1 - me, 1)

    def slot_of(t):
        v = t - (nf - 2 + LATE) + 3 * between + nf * (LEAD + 3)
        return lax.div(v, nf) - (LEAD + 3), lax.rem(v, nf)

    for n in range(min(LEAD, chunks)):
        b_head(n)

    def begin(s, carry):
        h_start(s)
        return carry

    lax.fori_loop(0, min(AHEAD, cases), begin, 0)
    for n in range(chunks):
        b_local(n).start()

    plane_time = h2.shape[1]
    total_time = plane_time * nf
    half = rows // 2
    unit = 2.0 * math.pi / total_time
    times = me * plane_time + lax.broadcasted_iota(jnp.int32, (half, plane_time), 1)
    bins = lax.broadcasted_iota(jnp.int32, (half, plane_time), 0) + 1
    scale = (0.5 - 0.5 * jnp.cos(unit * times[:8].astype(jnp.float32)))[:1] / math.sqrt(total_time)

    def tabulate(g, carry):
        angle = unit * lax.rem(times * (bins + g * half), total_time).astype(jnp.float32)
        for c, wave in enumerate((jnp.cos(angle) * scale, -jnp.sin(angle) * scale)):
            at = pl.ds(pl.multiple_of(g * rows + c * half, 16), half)
            high, low = split(wave)
            th[at, :] = high
            tl_[at, :] = low
        return carry

    with jax.named_scope('table'):
        lax.fori_loop(0, nf, tabulate, 0)

    def drain_inputs():
        def drain(s, carry):
            for d in range(1, np_):
                h_copy(s, lax.rem(p + d, np_), p).wait_send()
            for d in range(1, nf):
                @pl.when(me + d <= nf - 1)
                def _():
                    r_copy(s, me + d, me + d, right).wait_send()

                @pl.when(me - d >= 0)
                def _():
                    r_copy(s, me - d, me - d, left).wait_send()
            return carry

        lax.fori_loop(0, cases, drain, 0)
        for g in range(nf):
            @pl.when(jnp.logical_and(g <= me, has_r))
            def _():
                for n in range(chunks):
                    b_copy(g, n, right, b_send_r).wait_send()

            @pl.when(jnp.logical_and(g >= me, has_l))
            def _():
                for n in range(chunks):
                    b_copy(g, n, left, b_send_l).wait_send()

    def tick(step, carry):
        t = step - nf * LEAD
        i = lax.div(step, nf) - LEAD
        tau = lax.rem(step, nf)

        @pl.when(jnp.logical_and(tau == 0, jnp.logical_and(i >= 0, i < cases)))
        def _():
            if AHEAD < cases:
                @pl.when(i + AHEAD < cases)
                def _():
                    h_start(i + AHEAD)
            for d in range(1, np_):
                q = lax.rem(p + d, np_)
                h_copy(i, q, q).wait_recv()
            h_local(i).wait()
            with jax.named_scope('dft'):
              spec[lax.rem(i, RING)] = dot3((th[...], tl_[...]), split(h2[i]))
            wf[lax.rem(i, RING + 1)] = own(i, me)

        with jax.named_scope('send'):
            send(t)

        j, part = slot_of(t)
        live = jnp.logical_and(j >= 1, j <= cases)

        @pl.when(jnp.logical_and(part == 0, live))
        def _():
            @pl.when(j == 1)
            def _():
                for n in range(chunks):
                    b_local(n).wait()

            @pl.when(jnp.logical_or(jnp.logical_not(has_r), jnp.logical_not(has_l)))
            def _():
                def taken(n, carry):
                    take(n)
                    return carry

                lax.fori_loop(ready(j - 1) * jnp.minimum(j - 1, 1), ready(j), taken, 0)

            with jax.named_scope('fitB'):
                new_chunk(j, compute)
            with jax.named_scope('finalize'):
                finalize(j - 1)
        @pl.when(jnp.logical_and(part == 1, live))
        def _():
            with jax.named_scope('passB'):
                new_chunk(j, pass_on)
            with jax.named_scope('fitA'):
                new_case(j, compute)

        @pl.when(jnp.logical_and(part == 2, live))
        def _():
            with jax.named_scope('passA'):
                new_case(j, pass_on)

        @pl.when(jnp.logical_and(part == 2, j == cases + 1))
        def _():
            with jax.named_scope('drain'):
                drain_inputs()

        def relays(i, carry):
            new_chunk(i, relay)
            new_case(i, relay)
            return carry

        @pl.when(jnp.logical_and(part == 3, jnp.logical_and(j >= RELAY, j <= cases + 1)))
        def _():
            with jax.named_scope('relay'):
                lax.fori_loop((j - 1) * jnp.minimum(j - RELAY, 1) + (1 - jnp.minimum(j - RELAY, 1)), j, relays, 0)

        return carry

    lax.fori_loop(0, nf * (LEAD + cases + 2) + LATE + 2, tick, 0)

    total = cases * pieces

    def finish(e, carry):
        turn = lax.rem(lax.div(e, pieces) + lax.rem(e, pieces), 2)

        with jax.named_scope('fwait'):
            @pl.when(turn == 0)
            def _():
                acc = pland[e, chip] + landed(e, cy)
                for row in others():
                    acc = acc + landed(e, lines + row)
                pland[e, chip] = acc

            @pl.when(turn == 1)
            def _():
                acc = pland[e, chip]
                for row in others() + [cy]:
                    acc = acc + landed(e, row * 2)
                pland[e, chip] = acc

        o_copy(e).start()
        return carry

    with jax.named_scope('finish'):
        lax.fori_loop(0, total, finish, 0)

    def drain_out(e, carry):
        for d in range(1, chips):
            c = lax.rem(chip + d, chips)
            f_copy(e, c, c, chip).wait_send()
        o_copy(e).wait()
        return carry

    lax.fori_loop(0, total, drain_out, 0)


def local(histories, point_weight, basis):
    nf = lax.axis_size("freq")
    np_ = lax.axis_size("pts")
    cases, time_local, all_points = histories.shape
    points = all_points // np_
    plane_time = time_local * np_
    rows = 2 * F // nf
    ho = basis.shape[1] * nf // np_
    pieces = ho // COLS
    chunks = np_ // nf * pieces
    chips = np_ // 2
    total = cases * pieces
    slots = cases - 1 + chunks
    assert np_ == 2 * nf
    f32, bf16 = jnp.float32, jnp.bfloat16
    hbm = pl.BlockSpec(memory_space=pl.ANY)
    vmem = pl.BlockSpec(memory_space=pltpu.VMEM)
    dma = pltpu.SemaphoreType.DMA
    coeffs = pl.pallas_call(
        functools.partial(kernel, nf, np_),
        out_shape=jax.ShapeDtypeStruct((cases * rows, ho), f32),
        in_specs=[hbm, vmem, hbm],
        out_specs=hbm,
        scratch_shapes=[
            pltpu.VMEM((cases, plane_time, points), f32),
            pltpu.VMEM((np_, pieces, points, COLS), f32),
            pltpu.VMEM((cases, nf + 1, rows, points), f32),
            pltpu.VMEM((RING, 2 * F, points), f32),
            pltpu.VMEM((RING + 1, rows, points), f32),
            pltpu.VMEM((2 * F, plane_time), bf16),
            pltpu.VMEM((2 * F, plane_time), bf16),
            pltpu.VMEM((cases, rows, points), bf16),
            pltpu.VMEM((cases, rows, points), bf16),
            pltpu.VMEM((slots, chips, rows, COLS), f32),
            pltpu.VMEM((total, chips, rows, COLS), f32),
            pltpu.VMEM((total, chips, rows, COLS), f32),
            dma((cases, np_)), dma((cases, np_)), dma((cases,)),
            dma((nf, chunks)), dma((nf, chunks)), dma((nf, chunks)), dma((chunks,)),
            dma((cases, nf)), dma((cases, nf + 1)),
            dma((slots,)), dma((total,)),
            dma((total, chips)), dma((total, chips)), dma((total,)),
        ],
        compiler_params=pltpu.CompilerParams(
            collective_id=0, has_side_effects=True, vmem_limit_bytes=65000 * 1024
        ),
    )(histories, point_weight.reshape(1, -1), basis)
    return coeffs.reshape(cases, 2, rows // 2, ho)


def solution(mesh):
    return jax.shard_map(
        local,
        mesh=mesh,
        in_specs=(P(None, ("freq", "pts"), None), P("pts"), P("pts", "freq")),
        out_specs=P(None, None, "freq", "pts"),
        check_vma=False,
    )
```

time: 246 us -> 222 us (0.902)
  Pallas kernels: 239 us -> 218 us
  other arithmetic: 3.27 us -> 0 us
    pallas_call x1, Pallas kernels: 239 us -> 218 us  [local(): pl.pallas_call(functools.partial(kernel, nf, np_), out_shape=jax.ShapeDty...]
where the time goes in v1:
time: 222 us
  Pallas kernels  218 us (98%)
  local copies, waits for them, and re-layouts  3.14 us (1%)
    pallas_call x1, Pallas kernels, local(): pl.pallas_call(functools.partial(kernel, nf, np_), out_shape=jax.ShapeDty...  218 us

profile of v1, /device:TPU:1, one launch (start us, length us, event | category | flops | bytes accessed | tf_op | source)
XLA Modules:
  0.0 221.6 jit_solution(11523530472092890140)
XLA Ops:
  0.0 218.5 %shard_map.37 = f32[1024,512]{1,0:T(8,128)} custom-call(f32[8,64,4096]{2,1,0:T(8,128)} %hist.1, f32[1,512]{1,0:T(1,128)} %bitcast.3, f32[512,1024]{1,0:T(8,128)} %basis.1), custom_call_target="tpu_custom_call" | custom-call | tf_op jit(solution)/shard_map/pallas_call | solution.py:516
  218.5 3.1 %copy.5 = f32[8,2,64,512]{3,2,1,0:T(8,128)} copy(f32[8,2,64,512]{3,2,1,0:T(8,128)} %bitcast.2) | data formatting | bytes 4194304

commit v2 on v1

--- a/solution.py
+++ b/solution.py
@@ -13,6 +13,7 @@
 LATE = 2
 RELAY = 4
 AHEAD = 8
+BEHIND = 3
 COLS = 128
 RING = 2
 MESH = pl.DeviceIdType.MESH
@@ -32,13 +33,13 @@
 
 def kernel(
     nf, np_, hist, weight, basis, out,
-    h2, bas, rs, spec, wf, th, tl_, wh, wl, stage, pland, fland,
-    h_send, h_recv, h_own, b_send_r, b_send_l, b_recv, b_own,
+    h2, bas, rs, spec, wf, th, tl_, wt, stage, pland, fland,
+    h_send, h_recv, b_send_r, b_send_l, b_recv, b_own,
     r_send, r_recv, p_send, p_recv, f_send, f_recv, o_sem,
 ):
     cases, time_local, _ = hist.shape
     points = h2.shape[2]
-    rows = wh.shape[1]
+    rows = rs.shape[2]
     per = np_ // nf
     pieces = bas.shape[1]
     ho = pieces * COLS
@@ -77,7 +78,7 @@
         return pltpu.make_async_remote_copy(
             src_ref=hist.at[s, :, pl.ds(pl.multiple_of(q * points, 128), points)],
             dst_ref=h2.at[s, pl.ds(pl.multiple_of(slot * time_local, 8), time_local), :],
-            send_sem=h_send.at[s, q], recv_sem=h_recv.at[s, slot],
+            send_sem=h_send, recv_sem=h_recv.at[s],
             device_id={"pts": q}, device_id_type=MESH,
         )
 
@@ -85,8 +86,11 @@
         return pltpu.make_async_copy(
             hist.at[s, :, pl.ds(pl.multiple_of(p * points, 128), points)],
             h2.at[s, pl.ds(pl.multiple_of(p * time_local, 8), time_local), :],
-            h_own.at[s],
-        )
+            h_recv.at[s],
+        )
+
+    def whole_copy(ref, sem):
+        return pltpu.make_async_copy(ref, ref, sem)
 
     def h_start(s):
         for d in range(1, np_):
@@ -104,7 +108,7 @@
         dst = b_place(b, n)
         return pltpu.make_async_remote_copy(
             src_ref=dst if src is None else src, dst_ref=dst,
-            send_sem=sems.at[b, n], recv_sem=b_recv.at[b, n],
+            send_sem=sems.at[b], recv_sem=b_recv.at[b, n],
             device_id={"freq": to}, device_id_type=MESH,
         )
 
@@ -118,11 +122,11 @@
             b_copy(me, n, left, b_send_l, b_source(n)).start()
 
     def b_local(n):
-        return pltpu.make_async_copy(b_source(n), b_place(me, n), b_own.at[n])
+        return pltpu.make_async_copy(b_source(n), b_place(me, n), b_own)
 
     def r_copy(s, g, dst, to):
         return pltpu.make_async_remote_copy(
-            src_ref=rs.at[s, g], dst_ref=rs.at[s, dst], send_sem=r_send.at[s, g], recv_sem=r_recv.at[s, dst],
+            src_ref=rs.at[s, g], dst_ref=rs.at[s, dst], send_sem=r_send, recv_sem=r_recv.at[s, dst],
             device_id={"freq": to}, device_id_type=MESH,
         )
 
@@ -203,8 +207,8 @@
             wf[at] = wf[at] + rs[s, nf]
 
         high, low = split(wf[at] * weight[...])
-        wh[s] = high
-        wl[s] = low
+        wt[s, :rows] = high
+        wt[s, rows:] = low
 
     def p_copy(e, slot):
         return pltpu.make_async_remote_copy(
@@ -217,15 +221,14 @@
     cy, cx = lax.div(chip, 2), lax.rem(chip, 2)
     beside = cy * 2 + 1 - cx
 
-    def f_copy(e, c, to, slot):
+    def f_copy(e, c, to, slot, leg):
         return pltpu.make_async_remote_copy(
-            src_ref=pland.at[e, c], dst_ref=fland.at[e, slot], send_sem=f_send.at[e, c], recv_sem=f_recv.at[e, slot],
+            src_ref=pland.at[e, c], dst_ref=fland.at[e, slot], send_sem=f_send, recv_sem=f_recv.at[e, leg],
             device_id={"pts": to * 2 + core}, device_id_type=MESH,
         )
 
-    def landed(e, slot):
-        f_copy(e, beside, beside, slot).wait_recv()
-        return fland[e, slot]
+    def landed(e, leg):
+        whole_copy(fland.at[e, pl.ds(0, lines - 1 + leg)], f_recv.at[e, leg]).wait()
 
     def others():
         return [lax.rem(cy + d, lines) for d in range(1, lines)]
@@ -235,15 +238,18 @@
         return pltpu.make_async_copy(
             pland.at[e, chip],
             out.at[pl.ds(pl.multiple_of(s * rows, 8), rows), pl.ds(pl.multiple_of(m * COLS, 128), COLS)],
-            o_sem.at[e],
+            o_sem,
         )
 
     def compute(s, n, slot):
         m, target = lax.div(n, 2), lax.rem(n, 2)
-        lhs = wh[s], wl[s]
+        lhs = wt[s]
+        dot = functools.partial(jnp.dot, preferred_element_type=jnp.float32)
         for c in range(0, chips, 2):
             pair = jnp.concatenate([bas[c * 2 + target, m], bas[c * 2 + 2 + target, m]], axis=1)
-            both = dot3(lhs, split(pair))
+            high, low = split(pair)
+            tall = dot(lhs, high)
+            both = tall[:rows] + (dot(lhs[:rows], low) + tall[rows:])
             stage[slot, c] = both[:, :COLS]
             stage[slot, c + 1] = both[:, COLS:]
 
@@ -270,14 +276,15 @@
 
         @pl.when(turn == 0)
         def _():
-            for row in others() + [cy]:
-                f_copy(e, row * 2 + 1 - cx, beside, row).start()
+            for row in others():
+                f_copy(e, row * 2 + 1 - cx, beside, row, 0).start()
+            f_copy(e, beside, beside, cy, 1).start()
 
         @pl.when(turn == 1)
         def _():
             for row in others():
-                f_copy(e, row * 2 + 1 - cx, row * 2 + cx, cy * 2 + 1).start()
-                f_copy(e, row * 2 + cx, row * 2 + cx, cy * 2).start()
+                f_copy(e, row * 2 + 1 - cx, row * 2 + cx, cy * 2 + 1, 0).start()
+                f_copy(e, row * 2 + cx, row * 2 + cx, cy * 2, 1).start()
 
     def relay(s, n, slot):
         @pl.when(lax.rem(n, 2) == core)
@@ -287,19 +294,20 @@
     def turn_over(s, m):
         e = s * pieces + m
         turn = lax.rem(s + m, 2)
+        landed(e, 0)
 
         @pl.when(turn == 0)
         def _():
             for row in others():
                 c = row * 2 + cx
-                pland[e, c] = pland[e, c] + landed(e, row)
-                f_copy(e, c, c, lines + cy).start()
+                pland[e, c] = pland[e, c] + fland[e, row]
+                f_copy(e, c, c, lines + cy, 1).start()
 
         @pl.when(turn == 1)
         def _():
             for row in others():
-                pland[e, beside] = pland[e, beside] + landed(e, row * 2 + 1)
-            f_copy(e, beside, beside, cy * 2).start()
+                pland[e, beside] = pland[e, beside] + fland[e, row * 2 + 1]
+            f_copy(e, beside, beside, cy * 2, 1).start()
 
     def ready(i):
         return jnp.minimum(i + LEAD - 1, chunks)
@@ -314,12 +322,12 @@
 
         lax.fori_loop(ready(i - 1), ready(i), cases_of, 0)
 
-    def new_case(i, act):
+    def new_case(i, act, low=0):
         def one(n, carry):
             act(i - 1, n, cases - 1 + n)
             return carry
 
-        lax.fori_loop(0, ready(i), one, 0)
+        lax.fori_loop(low, ready(i), one, 0)
 
     between = jnp.minimum(me, 1) * jnp.minimum(nf - 1 - me, 1)
 
@@ -359,30 +367,18 @@
         lax.fori_loop(0, nf, tabulate, 0)
 
     def drain_inputs():
-        def drain(s, carry):
-            for d in range(1, np_):
-                h_copy(s, lax.rem(p + d, np_), p).wait_send()
-            for d in range(1, nf):
-                @pl.when(me + d <= nf - 1)
-                def _():
-                    r_copy(s, me + d, me + d, right).wait_send()
-
-                @pl.when(me - d >= 0)
-                def _():
-                    r_copy(s, me - d, me - d, left).wait_send()
-            return carry
-
-        lax.fori_loop(0, cases, drain, 0)
+        whole_copy(h2.at[:, pl.ds(0, time_local * (np_ - 1))], h_send).wait()
+        whole_copy(rs.at[:, pl.ds(0, nf - 1)], r_send).wait()
         for g in range(nf):
+            block = bas.at[pl.ds(g * per, per)]
+
             @pl.when(jnp.logical_and(g <= me, has_r))
             def _():
-                for n in range(chunks):
-                    b_copy(g, n, right, b_send_r).wait_send()
+                whole_copy(block, b_send_r.at[g]).wait()
 
             @pl.when(jnp.logical_and(g >= me, has_l))
             def _():
-                for n in range(chunks):
-                    b_copy(g, n, left, b_send_l).wait_send()
+                whole_copy(block, b_send_l.at[g]).wait()
 
     def tick(step, carry):
         t = step - nf * LEAD
@@ -395,10 +391,7 @@
                 @pl.when(i + AHEAD < cases)
                 def _():
                     h_start(i + AHEAD)
-            for d in range(1, np_):
-                q = lax.rem(p + d, np_)
-                h_copy(i, q, q).wait_recv()
-            h_local(i).wait()
+            whole_copy(h2.at[i], h_recv.at[i]).wait()
             with jax.named_scope('dft'):
               spec[lax.rem(i, RING)] = dot3((th[...], tl_[...]), split(h2[i]))
             wf[lax.rem(i, RING + 1)] = own(i, me)
@@ -413,8 +406,7 @@
         def _():
             @pl.when(j == 1)
             def _():
-                for n in range(chunks):
-                    b_local(n).wait()
+                whole_copy(bas.at[pl.ds(me * per, per)], b_own).wait()
 
             @pl.when(jnp.logical_or(jnp.logical_not(has_r), jnp.logical_not(has_l)))
             def _():
@@ -433,12 +425,19 @@
             with jax.named_scope('passB'):
                 new_chunk(j, pass_on)
             with jax.named_scope('fitA'):
-                new_case(j, compute)
+                def fit(s, n, slot):
+                    compute(s, n, slot)
+
+                    @pl.when(n >= BEHIND)
+                    def _():
+                        pass_on(s, n - BEHIND, slot - BEHIND)
+
+                new_case(j, fit)
 
         @pl.when(jnp.logical_and(part == 2, live))
         def _():
             with jax.named_scope('passA'):
-                new_case(j, pass_on)
+                new_case(j, pass_on, jnp.maximum(ready(j) - BEHIND, 0))
 
         @pl.when(jnp.logical_and(part == 2, j == cases + 1))
         def _():
@@ -464,20 +463,21 @@
     def finish(e, carry):
         turn = lax.rem(lax.div(e, pieces) + lax.rem(e, pieces), 2)
 
-        with jax.named_scope('fwait'):
-            @pl.when(turn == 0)
-            def _():
-                acc = pland[e, chip] + landed(e, cy)
-                for row in others():
-                    acc = acc + landed(e, lines + row)
-                pland[e, chip] = acc
-
-            @pl.when(turn == 1)
-            def _():
-                acc = pland[e, chip]
-                for row in others() + [cy]:
-                    acc = acc + landed(e, row * 2)
-                pland[e, chip] = acc
+        landed(e, 1)
+
+        @pl.when(turn == 0)
+        def _():
+            acc = pland[e, chip] + fland[e, cy]
+            for row in others():
+                acc = acc + fland[e, lines + row]
+            pland[e, chip] = acc
+
+        @pl.when(turn == 1)
+        def _():
+            acc = pland[e, chip]
+            for row in others() + [cy]:
+                acc = acc + fland[e, row * 2]
+            pland[e, chip] = acc
 
         o_copy(e).start()
         return carry
@@ -485,14 +485,9 @@
     with jax.named_scope('finish'):
         lax.fori_loop(0, total, finish, 0)
 
-    def drain_out(e, carry):
-        for d in range(1, chips):
-            c = lax.rem(chip + d, chips)
-            f_copy(e, c, c, chip).wait_send()
-        o_copy(e).wait()
-        return carry
-
-    lax.fori_loop(0, total, drain_out, 0)
+    with jax.named_scope('drain_out'):
+        whole_copy(pland.at[:, pl.ds(0, chips - 1)], f_send).wait()
+        whole_copy(pland.at[:, 0], o_sem).wait()
 
 
 def local(histories, point_weight, basis):
@@ -526,16 +521,15 @@
             pltpu.VMEM((RING + 1, rows, points), f32),
             pltpu.VMEM((2 * F, plane_time), bf16),
             pltpu.VMEM((2 * F, plane_time), bf16),
-            pltpu.VMEM((cases, rows, points), bf16),
-            pltpu.VMEM((cases, rows, points), bf16),
+            pltpu.VMEM((cases, 2 * rows, points), bf16),
             pltpu.VMEM((slots, chips, rows, COLS), f32),
             pltpu.VMEM((total, chips, rows, COLS), f32),
             pltpu.VMEM((total, chips, rows, COLS), f32),
-            dma((cases, np_)), dma((cases, np_)), dma((cases,)),
-            dma((nf, chunks)), dma((nf, chunks)), dma((nf, chunks)), dma((chunks,)),
-            dma((cases, nf)), dma((cases, nf + 1)),
+            dma, dma((cases,)),
+            dma((nf,)), dma((nf,)), dma((nf, chunks)), dma,
+            dma, dma((cases, nf + 1)),
             dma((slots,)), dma((total,)),
-            dma((total, chips)), dma((total, chips)), dma((total,)),
+            dma, dma((total, 2)), dma,
         ],
         compiler_params=pltpu.CompilerParams(
             collective_id=0, has_side_effects=True, vmem_limit_bytes=65000 * 1024

time: 222 us -> 218 us (0.982)
  Pallas kernels: 218 us -> 214 us
    pallas_call x1, Pallas kernels: 218 us -> 214 us  [local(): pl.pallas_call(functools.partial(kernel, nf, np_), out_shape=jax.ShapeDty...]
where the time goes in v2:
time: 218 us; the launch traced here: 217 us
  Pallas kernels  214 us (98%)
  local copies, waits for them, and re-layouts  3.14 us (1%)
    pallas_call x1, Pallas kernels, local(): pl.pallas_call(functools.partial(kernel, nf, np_), out_shape=jax.ShapeDty...  214 us

profile of v2, /device:TPU:1, one launch (start us, length us, event | category | flops | bytes accessed | tf_op | source)
XLA Modules:
  0.0 217.5 jit_solution(8377036498068093419)
XLA Ops:
  0.0 214.3 %shard_map.37 = f32[1024,512]{1,0:T(8,128)} custom-call(f32[8,64,4096]{2,1,0:T(8,128)} %hist.1, f32[1,512]{1,0:T(1,128)} %bitcast.3, f32[512,1024]{1,0:T(8,128)} %basis.1), custom_call_target="tpu_custom_call" | custom-call | tf_op jit(solution)/shard_map/pallas_call | solution.py:511
  214.3 3.1 %copy.5 = f32[8,2,64,512]{3,2,1,0:T(8,128)} copy(f32[8,2,64,512]{3,2,1,0:T(8,128)} %bitcast.2) | data formatting | bytes 4194304

commit v3 on v2

--- a/solution.py
+++ b/solution.py
@@ -402,6 +402,16 @@
         j, part = slot_of(t)
         live = jnp.logical_and(j >= 1, j <= cases)
 
+        def relays(i, carry):
+            new_chunk(i, relay)
+            new_case(i, relay)
+            return carry
+
+        @pl.when(jnp.logical_and(part == 0, j == cases))
+        def _():
+            with jax.named_scope('relayB'):
+                lax.fori_loop(cases - 1, cases, relays, 0)
+
         @pl.when(jnp.logical_and(part == 0, live))
         def _():
             @pl.when(j == 1)
@@ -444,12 +454,7 @@
             with jax.named_scope('drain'):
                 drain_inputs()
 
-        def relays(i, carry):
-            new_chunk(i, relay)
-            new_case(i, relay)
-            return carry
-
-        @pl.when(jnp.logical_and(part == 3, jnp.logical_and(j >= RELAY, j <= cases + 1)))
+        @pl.when(jnp.logical_and(jnp.logical_and(part == 3, j != cases), jnp.logical_and(j >= RELAY, j <= cases + 1)))
         def _():
             with jax.named_scope('relay'):
                 lax.fori_loop((j - 1) * jnp.minimum(j - RELAY, 1) + (1 - jnp.minimum(j - RELAY, 1)), j, relays, 0)

time: 218 us -> 217 us (level)
  no operation moved by 1% of the time
where the time goes in v3:
time: 217 us
  Pallas kernels  214 us (99%)
  local copies, waits for them, and re-layouts  3.14 us (1%)
    pallas_call x1, Pallas kernels, local(): pl.pallas_call(functools.partial(kernel, nf, np_), out_shape=jax.ShapeDty...  214 us

profile of v3, /device:TPU:1, one launch (start us, length us, event | category | flops | bytes accessed | tf_op | source)
XLA Modules:
  0.0 217.2 jit_solution(7931373490042465773)
XLA Ops:
  0.0 214.0 %shard_map.37 = f32[1024,512]{1,0:T(8,128)} custom-call(f32[8,64,4096]{2,1,0:T(8,128)} %hist.1, f32[1,512]{1,0:T(1,128)} %bitcast.3, f32[512,1024]{1,0:T(8,128)} %basis.1), custom_call_target="tpu_custom_call" | custom-call | tf_op jit(solution)/shard_map/pallas_call | solution.py:516
  214.0 3.1 %copy.5 = f32[8,2,64,512]{3,2,1,0:T(8,128)} copy(f32[8,2,64,512]{3,2,1,0:T(8,128)} %bitcast.2) | data formatting | bytes 4194304
